TPU v7x, 32 devices: a whole 2x2x4 slice. The times are simulated.
32 devices in a mesh: dp: 4 (over y, x), mp: 8 (over z, core).
Axes of the slice: x: 2, y: 2, z: 4, core: 2. Of those that a mesh axis runs over, the one named last changes fastest.
Arguments:
- tokens: bfloat16 [4096, 2048], P(('dp', 'mp')), may hold values from -9 to 9
- seg_ids: int32 [4096], P('dp'), may hold values from 0 to 12, as said below
- positions: int32 [4096], P('dp'), may hold values from 0 to 1023, as said below
- w_query: bfloat16 [2048, 2048], P(None, 'mp'), may hold values from -0.125 to 0.125
- w_key: bfloat16 [2048, 512], replicated, may hold values from -0.125 to 0.125
- w_value: bfloat16 [2048, 512], replicated, may hold values from -0.125 to 0.125
- w_output: bfloat16 [2048, 2048], P('mp'), may hold values from -0.75 to 0.75
- w_gate: bfloat16 [2048, 8192], P(None, 'mp'), may hold values from -0.125 to 0.125
- w_up: bfloat16 [2048, 8192], P(None, 'mp'), may hold values from -0.125 to 0.125
- w_down: bfloat16 [8192, 2048], P('mp'), may hold values from -0.0625 to 0.0625
- attn_gain: float32 [2048], replicated, may hold values from 0.5 to 1.5
- ffn_gain: float32 [2048], replicated, may hold values from 0.5 to 1.5
- query_gain: float32 [64], replicated, may hold values from 0.1 to 1.9
- key_gain: float32 [64], replicated, may hold values from 0.1 to 1.9
- out_grad: bfloat16 [4096, 2048], P(('dp', 'mp')), may hold values from -6 to 6
Outputs:
- output: bfloat16 [4096, 2048], P(('dp', 'mp'))
- grad_tokens: bfloat16 [4096, 2048], P(('dp', 'mp'))
- grad_w_query: float32 [2048, 2048], P(None, 'mp')
- grad_w_key: float32 [2048, 512], replicated
- grad_w_value: float32 [2048, 512], replicated
- grad_w_output: float32 [2048, 2048], P('mp')
- grad_w_gate: float32 [2048, 8192], P(None, 'mp')
- grad_w_up: float32 [2048, 8192], P(None, 'mp')
- grad_w_down: float32 [8192, 2048], P('mp')
- grad_attn_gain: float32 [2048], replicated
- grad_ffn_gain: float32 [2048], replicated
- grad_query_gain: float32 [64], replicated
- grad_key_gain: float32 [64], replicated
- residual_rms: float32 [1], replicated
- branch_rms: float32 [2, 4096], P(None, ('dp', 'mp'))
Inputs may be any that keep to these rules, and one draw needn't show every extreme that they name: `seg_ids`: never falling along the tokens; the first token of every block of 1024 consecutive tokens starts a new segment; the first block is one segment, every other block holds exactly 4. `positions`: 0 at the first token of a segment, one more at each following token of it.
All inputs are finite; a program needn't handle non-finite values.
Results may differ from a plain program's by a relative error of at most 0.015.
Values may be sent and summed in bfloat16 or wider, within the bound.
A program may use at most 256 MiB of HBM per device.

v0:
```python
import jax
import jax.numpy as jnp
from jax import lax
from jax.sharding import PartitionSpec as P

HEADS = 32
KV = 8
HD = 64
EPSILON = 1e-06
ROPE_BASE = 10000.0
MASKED = -1e30


def matmul(left, right):
    return jnp.dot(left, right, preferred_element_type=jnp.float32)


def matmul_left_t(left, right):
    return lax.dot_general(
        left, right, (((0,), (0,)), ((), ())), preferred_element_type=jnp.float32
    )


def matmul_right_t(left, right):
    return lax.dot_general(
        left, right, (((1,), (1,)), ((), ())), preferred_element_type=jnp.float32
    )


def rope_tables(position_row):
    half = HD // 2
    freq = ROPE_BASE ** (-jnp.arange(half, dtype=jnp.float32) / half)
    angle = position_row.astype(jnp.float32)[:, None] * freq[None, :]
    return (jnp.cos(angle)[:, None, :], jnp.sin(angle)[:, None, :])


def rotate(values, cosine, sine):
    half = HD // 2
    first_half = values[..., :half]
    second_half = values[..., half:]
    return jnp.concatenate(
        [first_half * cosine - second_half * sine, second_half * cosine + first_half * sine], -1
    )


def unrotate(grads, cosine, sine):
    half = HD // 2
    first_half = grads[..., :half]
    second_half = grads[..., half:]
    return jnp.concatenate(
        [first_half * cosine + second_half * sine, second_half * cosine - first_half * sine], -1
    )


def norm_back(grad_normed, unit, inverse, gain):
    scaled = grad_normed * gain
    return inverse * (scaled - unit * jnp.mean(scaled * unit, -1, keepdims=True))


def per_device(
    tokens,
    seg_ids,
    positions,
    w_query,
    w_key,
    w_value,
    w_output,
    w_gate,
    w_up,
    w_down,
    attn_gain,
    ffn_gain,
    query_gain,
    key_gain,
    out_grad,
):
    tok_count = tokens.shape[0]
    model_width = tokens.shape[1]
    row_count = tok_count * lax.axis_size("mp")
    query_width = w_query.shape[1]
    heads_dev = query_width // HD
    ffn_width = w_gate.shape[1]
    group = lax.axis_index("mp") * heads_dev // (HEADS // KV)
    score_scale = HD ** (-0.5)
    tokens_f = tokens.astype(jnp.float32)
    inv_one = lax.rsqrt(jnp.mean(tokens_f * tokens_f, -1, keepdims=True) + EPSILON)
    normed_one = tokens_f * inv_one
    h_one = (normed_one * attn_gain).astype(jnp.bfloat16)
    key_cols = lax.dynamic_slice_in_dim(w_key, group * HD, HD, 1)
    value_cols = lax.dynamic_slice_in_dim(w_value, group * HD, HD, 1)
    w_attn = jnp.concatenate([w_query, key_cols, value_cols], 1)
    gathered_one = lax.all_gather(h_one, "mp", axis=0, tiled=True)
    projected = matmul(gathered_one, w_attn)
    query = projected[:, :query_width].reshape(row_count, heads_dev, HD)
    key_proj = projected[:, query_width : query_width + HD]
    value_low = projected[:, query_width + HD :].astype(jnp.bfloat16)
    query_inv = lax.rsqrt(jnp.mean(query * query, -1, keepdims=True) + EPSILON)
    query_unit = query * query_inv
    key_inv = lax.rsqrt(jnp.mean(key_proj * key_proj, -1, keepdims=True) + EPSILON)
    key_unit = key_proj * key_inv
    cosine, sine = rope_tables(positions)
    query_rot = rotate(query_unit * query_gain, cosine, sine).astype(jnp.bfloat16)
    key_rot = rotate((key_unit * key_gain)[:, None, :], cosine, sine)[:, 0, :].astype(jnp.bfloat16)
    block = min(512, row_count)
    block_count = row_count // block
    token_index = jnp.arange(row_count, dtype=jnp.int32)
    starts = jnp.arange(block_count, dtype=jnp.int32) * block
    query_blocks = query_rot.reshape(block_count, block, heads_dev, HD)

    def block_scores(query_block, start):
        scores = (
            jnp.einsum("qhd,kd->hqk", query_block, key_rot, preferred_element_type=jnp.float32)
            * score_scale
        )
        segment_block = lax.dynamic_slice_in_dim(seg_ids, start, block)
        index_block = start + jnp.arange(block, dtype=jnp.int32)
        allowed = (segment_block[:, None] == seg_ids[None, :]) & (
            token_index[None, :] <= index_block[:, None]
        )
        return jnp.where(allowed[None], scores, MASKED)

    def forward_block(inputs):
        query_block, start = inputs
        scores = block_scores(query_block, start)
        top = jnp.max(scores, -1, keepdims=True)
        expo = jnp.exp(scores - top)
        total = jnp.sum(expo, -1, keepdims=True)
        probs = (expo / total).astype(jnp.bfloat16)
        context_block = jnp.einsum(
            "hqk,kd->qhd", probs, value_low, preferred_element_type=jnp.float32
        )
        return (context_block.astype(jnp.bfloat16), (top + jnp.log(total))[..., 0])

    context_blocks, lse_blocks = lax.map(forward_block, (query_blocks, starts))
    context = context_blocks.reshape(row_count, query_width)
    attn_branch = lax.psum_scatter(matmul(context, w_output), "mp", scatter_dimension=0, tiled=True)
    residual_mid = tokens_f + attn_branch
    inv_two = lax.rsqrt(jnp.mean(residual_mid * residual_mid, -1, keepdims=True) + EPSILON)
    normed_two = residual_mid * inv_two
    h_two = (normed_two * ffn_gain).astype(jnp.bfloat16)
    w_ffn = jnp.concatenate([w_gate, w_up], 1)
    gathered_two = lax.all_gather(h_two, "mp", axis=0, tiled=True)
    gate_up = matmul(gathered_two, w_ffn)
    gate = gate_up[:, :ffn_width]
    up = gate_up[:, ffn_width:]
    sigma = jax.nn.sigmoid(gate)
    silu_gate = gate * sigma
    hidden = (silu_gate * up).astype(jnp.bfloat16)
    ffn_branch = lax.psum_scatter(
        matmul(hidden, w_down).astype(jnp.bfloat16), "mp", scatter_dimension=0, tiled=True
    ).astype(jnp.float32)
    output = (residual_mid + ffn_branch).astype(jnp.bfloat16)
    branch_rms = jnp.stack(
        [
            jnp.sqrt(jnp.mean(attn_branch * attn_branch, -1)),
            jnp.sqrt(jnp.mean(ffn_branch * ffn_branch, -1)),
        ]
    )
    squares_local = jnp.sum(tokens_f * tokens_f)
    squares_total = lax.psum(squares_local, ("dp", "mp"))
    grad_out = out_grad.astype(jnp.float32)
    grad_ffn_rows = lax.all_gather(out_grad, "mp", axis=0, tiled=True)
    grad_hidden = matmul_right_t(grad_ffn_rows, w_down)
    grad_w_down = matmul_left_t(hidden, grad_ffn_rows)
    grad_gate = grad_hidden * up * sigma * (1.0 + gate * (1.0 - sigma))
    grad_up = grad_hidden * silu_gate
    grad_gate_up = jnp.concatenate([grad_gate, grad_up], 1).astype(jnp.bfloat16)
    grad_w_ffn = matmul_left_t(gathered_two, grad_gate_up)
    grad_h_two = lax.psum_scatter(
        matmul_right_t(grad_gate_up, w_ffn), "mp", scatter_dimension=0, tiled=True
    )
    grad_ffn_gain = jnp.sum(grad_h_two * normed_two, 0)
    grad_mid = grad_out + norm_back(grad_h_two, normed_two, inv_two, ffn_gain)
    grad_attn_rows = lax.all_gather(grad_mid.astype(jnp.bfloat16), "mp", axis=0, tiled=True)
    grad_w_output = matmul_left_t(context, grad_attn_rows)
    grad_context = matmul_right_t(grad_attn_rows, w_output).astype(jnp.bfloat16)
    grad_context_blocks = grad_context.reshape(block_count, block, heads_dev, HD)

    def backward_block(carry, inputs):
        grad_key_acc, grad_value_acc = carry
        query_block, grad_block, lse_block, start = inputs
        scores = block_scores(query_block, start)
        exact = jnp.exp(scores - lse_block[..., None])
        grad_probs = jnp.einsum(
            "qhd,kd->hqk", grad_block, value_low, preferred_element_type=jnp.float32
        )
        delta = jnp.sum(exact * grad_probs, -1, keepdims=True)
        grad_scores = (exact * (grad_probs - delta)).astype(jnp.bfloat16)
        grad_query_block = (
            jnp.einsum("hqk,kd->qhd", grad_scores, key_rot, preferred_element_type=jnp.float32)
            * score_scale
        )
        grad_key_acc = (
            grad_key_acc
            + jnp.einsum(
                "hqk,qhd->kd", grad_scores, query_block, preferred_element_type=jnp.float32
            )
            * score_scale
        )
        grad_value_acc = grad_value_acc + jnp.einsum(
            "hqk,qhd->kd",
            exact.astype(jnp.bfloat16),
            grad_block,
            preferred_element_type=jnp.float32,
        )
        return ((grad_key_acc, grad_value_acc), grad_query_block)

    zero_rows = jnp.zeros((row_count, HD), jnp.float32)
    (grad_key_rot, grad_value), grad_query_blocks = lax.scan(
        backward_block,
        (zero_rows, zero_rows),
        (query_blocks, grad_context_blocks, lse_blocks, starts),
    )
    grad_query_rot = grad_query_blocks.reshape(row_count, heads_dev, HD)
    grad_query_normed = unrotate(grad_query_rot, cosine, sine)
    grad_key_normed = unrotate(grad_key_rot[:, None, :], cosine, sine)[:, 0, :]
    grad_query_gain = jnp.sum(grad_query_normed * query_unit, (0, 1))
    grad_key_gain = jnp.sum(grad_key_normed * key_unit, 0)
    grad_query = norm_back(grad_query_normed, query_unit, query_inv, query_gain)
    grad_key = norm_back(grad_key_normed, key_unit, key_inv, key_gain)
    grad_proj = jnp.concatenate(
        [grad_query.reshape(row_count, query_width), grad_key, grad_value], 1
    ).astype(jnp.bfloat16)
    grad_w_attn = matmul_left_t(gathered_one, grad_proj)
    grad_h_one = lax.psum_scatter(
        matmul_right_t(grad_proj, w_attn), "mp", scatter_dimension=0, tiled=True
    )
    grad_attn_gain = jnp.sum(grad_h_one * normed_one, 0)
    grad_tokens = (grad_mid + norm_back(grad_h_one, normed_one, inv_one, attn_gain)).astype(
        jnp.bfloat16
    )
    grad_w_query = grad_w_attn[:, :query_width]
    key_zeros = jnp.zeros(w_key.shape, jnp.float32)
    grad_w_key = lax.dynamic_update_slice_in_dim(
        key_zeros, grad_w_attn[:, query_width : query_width + HD], group * HD, 1
    )
    grad_w_value = lax.dynamic_update_slice_in_dim(
        key_zeros, grad_w_attn[:, query_width + HD :], group * HD, 1
    )
    grad_w_gate = grad_w_ffn[:, :ffn_width]
    grad_w_up = grad_w_ffn[:, ffn_width:]
    summed = lax.psum((grad_w_query, grad_w_output, grad_w_gate, grad_w_up, grad_w_down), "dp")
    shared = lax.psum(
        (grad_w_key, grad_w_value, grad_attn_gain, grad_ffn_gain, grad_query_gain, grad_key_gain),
        ("dp", "mp"),
    )
    entry_count = tok_count * model_width * lax.axis_size("dp") * lax.axis_size("mp")
    residual_rms = jnp.sqrt(squares_total / entry_count).reshape(1)
    return (
        output,
        grad_tokens,
        summed[0],
        shared[0],
        shared[1],
        summed[1],
        summed[2],
        summed[3],
        summed[4],
        shared[2],
        shared[3],
        shared[4],
        shared[5],
        residual_rms,
        branch_rms,
    )


def solution(mesh):
    return jax.shard_map(
        per_device,
        mesh=mesh,
        in_specs=(
            P(("dp", "mp"), None),
            P("dp"),
            P("dp"),
            P(None, "mp"),
            P(),
            P(),
            P("mp", None),
            P(None, "mp"),
            P(None, "mp"),
            P("mp", None),
            P(),
            P(),
            P(),
            P(),
            P(("dp", "mp"), None),
        ),
        out_specs=(
            P(("dp", "mp"), None),
            P(("dp", "mp"), None),
            P(None, "mp"),
            P(),
            P(),
            P("mp", None),
            P(None, "mp"),
            P(None, "mp"),
            P("mp", None),
            P(),
            P(),
            P(),
            P(),
            P(),
            P(None, ("dp", "mp")),
        ),
        check_vma=False,
    )
```

profile of v0, /device:TPU:0, one launch (start us, length us, event | category | flops | bytes accessed | tf_op | source)
XLA Modules:
  0.0 1435.8 jit_solution(14209004250411522282)
XLA Ops:
  15.5 45.7 %all-gather.5.cloned.1.call-done = bf16[1024,2048]{1,0:T(8,128)(2,1)} async-done(((bf16[128,2048]{1,0:T(8,128)(2,1)}), bf16[1024,2048]{1,0:T(8,128)(2,1)}) %all-gather.5.cloned.1.call-update) | async-done | bytes 4194320 | tf_op jit(solution)/shard_map/all_gather | solution.py:92
  70.9 25.0 %while.28 = (s32[]{:T(128)}, bf16[2,512,4,64]{1,3,2,0:T(8,128)(2,1)}, f32[2,4,512]{2,1,0:T(4,128)}, s32[2]{0:T(128)}, s32[1024]{0:T(1024)S(1)}, /*index=5*/bf16[...) while((s32[]{:T(128)}, ...), condition=%wide.region_6.7_spmd.clone, body=%wide.region_3.6_spmd.clone.sunk | while | flops 563739136 | bytes 32454952 | solution.py:134
  102.9 88.0 %reduce-scatter.5.cloned.1.call-done = f32[128,2048]{1,0:T(8,128)} async-done(((f32[1024,2048]{1,0:T(8,128)}), f32[128,2048]{1,0:T(8,128)}) %reduce-scatter.5.cloned.1.call-update) | async-done | bytes 1048592 | tf_op jit(solution)/shard_map/reduce_scatter | solution.py:136
  202.0 37.7 %all-gather.7.cloned.1.call-done = bf16[1024,2048]{1,0:T(8,128)(2,1)} async-done(((bf16[128,2048]{1,0:T(8,128)(2,1)}), bf16[1024,2048]{1,0:T(8,128)(2,1)}) %all-gather.7.cloned.1.call-update) | async-done | bytes 4194320 | tf_op jit(solution)/shard_map/all_gather | solution.py:142
  239.7 14.5 %fusion.103 = f32[1024,2048]{1,0:T(8,128)} fusion(bf16[1024,2048]{1,0:T(8,128)(2,1)} %all-gather.7.cloned.1.call-done, bf16[2048,2048]{1,0:T(8,128)(2,1)} %constant_dynamic-update-slice_fusion), kind=kOutput, calls=%fused_computation.175 | convolution fusion | flops 8589934592 | bytes 20971520 | tf_op jit(solution)/shard_map/dot_general | solution.py:15
  254.2 33.1 %all-gather.9.cloned.1.call-done = bf16[1024,2048]{1,0:T(8,128)(2,1)} async-done(((bf16[128,2048]{1,0:T(8,128)(2,1)}), bf16[1024,2048]{1,0:T(8,128)(2,1)}) %all-gather.9.cloned.1.call-update) | async-done | bytes 4194320 | tf_op jit(solution)/shard_map/all_gather | solution.py:162
  287.2 13.1 multiply_convert_fusion.1
  302.4 13.3 fusion.58
  315.9 88.1 %reduce-scatter.9.cloned.1.call-done = f32[128,2048]{1,0:T(8,128)} async-done(((f32[1024,2048]{1,0:T(8,128)}), f32[128,2048]{1,0:T(8,128)}) %reduce-scatter.9.cloned.1.call-update) | async-done | bytes 1048592 | tf_op jit(solution)/shard_map/reduce_scatter | solution.py:169
  409.3 44.9 %all-gather.11.cloned.1.call-done = bf16[1024,2048]{1,0:T(8,128)(2,1)} async-done(((bf16[128,2048]{1,0:T(8,128)(2,1)}), bf16[1024,2048]{1,0:T(8,128)(2,1)}) %all-gather.11.cloned.1.call-update) | async-done | bytes 4194320 | tf_op jit(solution)/shard_map/all_gather | solution.py:174
  459.4 80.9 %while.29 = (s32[]{:T(128)}, f32[1024,64]{0,1:T(8,128)S(1)}, f32[1024,64]{0,1:T(8,128)}, f32[2,512,4,64]{1,0,3,2:T(2,128)}, s32[2]{0:T(128)S(1)}, /*index=5*/s32...) while((s32[]{:T(128)}, f32[1024,64]{0,1:T(8,128)S(1)}, ...), condition=%wide.region_14.15_spmd.clone, body=%wide.region_12.14_spmd.clone.sunk | while | flops 1375664640 | bytes 114825640 | solution.py:209
  489.4 10.4 dynamic_update_slice.30
  521.1 5.9 fusion.162
  529.7 10.4 dynamic_update_slice.30
  555.3 9.3 convolution_convert_fusion
  565.1 10.8 fusion.105
  576.0 11.8 fusion.57
  587.8 6.8 fusion.100
  622.6 21.1 %reduce-scatter.11.cloned.1.call-done = f32[128,2048]{1,0:T(8,128)} async-done(((f32[1024,2048]{1,0:T(8,128)}), f32[128,2048]{1,0:T(8,128)}) %reduce-scatter.11.cloned.1.call-update) | async-done | bytes 1048592 | tf_op jit(solution)/shard_map/reduce_scatter | solution.py:225
  646.0 40.0 %all-reduce = (f32[2048]{0:T(1024)}, f32[2048]{0:T(1024)}, f32[64]{0:T(128)}, f32[64]{0:T(128)}, f32[]{:T(128)}) all-reduce(f32[2048]{0:T(1024)S(1)} %get-tuple-element.286, f32[2048]{0:T(1024)S(1)} %copy-done.44, f32[64]{0:T(128)S(1)} %reduce_sum.172, f32[64]{0:T(128)S(1)} %copy-done.55, ...), channel_id=1, replica_groups=mesh['dp'=4,'mp'=8] {'dp','mp'}, use_global_device_ids=true, to_apply=%region_27.28 | all-reduce | flops 4225 | bytes 33800 | tf_op jit(solution)/shard_map/psum | solution.py:243
  686.7 9.3 reduce-scatter.7.cloned.1.call-done
  699.7 514.7 %all-reduce.8.cloned.1.call-done = (f32[2048,256]{0,1:T(8,128)}, f32[256,2048]{1,0:T(8,128)}, f32[2048,1024]{1,0:T(8,128)}, f32[2048,1024]{1,0:T(8,128)}, f32[1024,2048]{1,0:T(8,128)}) async-done(((f32[2048,256]{0,1:T(8,128)}, f32[256,2048]{1,0:T(8,128)}, f32[2048,1024]{1,0:T(8,128)}, f32[2048,1024]{1,0:T(8,128)}, f32[1024,2048]{1,0:T(8,128)}), (f32[2048,256]{0,1:T(8,128)}, f32[256,2048]{1,0:T(8,128)}, ...) | async-done | bytes 29360144 | tf_op jit(solution)/shard_map/psum | solution.py:242
  1217.2 183.4 %all-reduce.6.cloned.1.call-done = (f32[2048,512]{1,0:T(8,128)}, f32[2048,512]{1,0:T(8,128)}) async-done(((f32[2048,512]{1,0:T(8,128)}, f32[2048,512]{1,0:T(8,128)}), (f32[2048,512]{1,0:T(8,128)}, f32[2048,512]{1,0:T(8,128)})) %all-reduce.6.cloned.1.call-update) | async-done | bytes 8388624 | tf_op jit(solution)/shard_map/psum | solution.py:243
  1409.9 9.1 copy.120
  (300 shorter events, 189.2 us)
Async XLA Ops:
  7.2 90.5 %copy-start = (bf16[256,2048]{1,0:T(8,128)(2,1)S(1)}, bf16[256,2048]{1,0:T(8,128)(2,1)}, u32[]{:S(2)}) copy-start(bf16[256,2048]{1,0:T(8,128)(2,1)} %param.25) | copy-start | bytes 3145732
  7.2 54.0 %all-gather.5.cloned.1.call-start = ((), (), s32[]{:S(2)}) async-start(), calls=%async_computation.4 | async-start | bytes 4718592 | tf_op jit(solution)/shard_map/all_gather | solution.py:92
  11.2 179.7 %reduce-scatter.5.cloned.1.call-start = ((), (), s32[]{:S(2)}) async-start(), calls=%async_computation.5 | async-start | bytes 9437184 | tf_op jit(solution)/shard_map/reduce_scatter | solution.py:136
  102.4 88.5 %copy-start.7 = (bf16[128,2048]{1,0:T(8,128)(2,1)S(1)}, bf16[128,2048]{1,0:T(8,128)(2,1)}, u32[]{:S(2)}) copy-start(bf16[128,2048]{1,0:T(8,128)(2,1)} %param.19) | copy-start | bytes 1572868
  102.4 90.5 %copy-start.36 = (f32[2048]{0:T(1024)S(1)}, f32[2048]{0:T(1024)}, u32[]{:S(2)}) copy-start(f32[2048]{0:T(1024)} %param.30) | copy-start | bytes 24580
  102.4 137.3 %all-gather.7.cloned.1.call-start = ((), (), s32[]{:S(2)}) async-start(), calls=%async_computation.6 | async-start | bytes 4718592 | tf_op jit(solution)/shard_map/all_gather | solution.py:142
  192.9 213.3 %copy-start.3 = (f32[128,2048]{1,0:T(8,128)}, f32[128,2048]{1,0:T(8,128)S(1)}, u32[]{:S(2)}) copy-start(f32[128,2048]{1,0:T(8,128)S(1)} %get-tuple-element.340) | copy-start | bytes 3145732
  192.9 213.3 %copy-start.45 = (f32[128]{0:T(128)}, f32[128]{0:T(128)S(1)}, u32[]{:S(2)}) copy-start(f32[128]{0:T(128)S(1)} %add_rsqrt_fusion.2) | copy-start | bytes 1540
  194.1 93.2 %all-gather.9.cloned.1.call-start = ((), (), s32[]{:S(2)}) async-start(), calls=%async_computation.8 | async-start | bytes 4718592 | tf_op jit(solution)/shard_map/all_gather | solution.py:162
  194.6 209.4 %reduce-scatter.9.cloned.1.call-start = ((), (), s32[]{:S(2)}) async-start(), calls=%async_computation.9 | async-start | bytes 9437184 | tf_op jit(solution)/shard_map/reduce_scatter | solution.py:169
  315.7 90.5 %copy-start.12 = (bf16[128,2048]{1,0:T(8,128)(2,1)S(1)}, bf16[128,2048]{1,0:T(8,128)(2,1)}, u32[]{:S(2)}) copy-start(bf16[128,2048]{1,0:T(8,128)(2,1)} %param.33) | copy-start | bytes 1572868
  315.7 93.0 %copy-start.51 = (f32[64]{0:T(128)S(1)}, f32[64]{0:T(128)}, u32[]{:S(2)}) copy-start(f32[64]{0:T(128)} %param.31) | copy-start | bytes 772
  315.7 138.5 %all-gather.11.cloned.1.call-start = ((), (), s32[]{:S(2)}) async-start(), calls=%async_computation.10 | async-start | bytes 4718592 | tf_op jit(solution)/shard_map/all_gather | solution.py:174
  408.6 235.2 %reduce-scatter.11.cloned.1.call-start = ((), (), s32[]{:S(2)}) async-start(), calls=%async_computation.11 | async-start | bytes 9437184 | tf_op jit(solution)/shard_map/reduce_scatter | solution.py:225
  459.4 83.9 %copy-start.6 = (f32[1024,384]{0,1:T(8,128)S(1)}, f32[1024,384]{0,1:T(8,128)}, u32[]{:S(2)}) copy-start(f32[1024,384]{0,1:T(8,128)} %copy-done.5) | copy-start | bytes 4718596
  555.3 140.8 %reduce-scatter.7.cloned.1.call-start = ((), (), s32[]{:S(2)}) async-start(), calls=%async_computation.7 | async-start | bytes 4718592 | tf_op jit(solution)/shard_map/reduce_scatter | solution.py:149
  564.7 649.7 %all-reduce.8.cloned.1.call-start = ((), (), s32[]{:S(2)}) async-start(), calls=%async_computation.13 | async-start | bytes 58720256 | tf_op jit(solution)/shard_map/psum | solution.py:242
  602.9 797.7 %all-reduce.6.cloned.1.call-start = ((), (), s32[]{:S(2)}) async-start(), calls=%async_computation.12 | async-start | bytes 16777216 | tf_op jit(solution)/shard_map/psum | solution.py:243
  621.9 74.1 %copy-start.4 = (f32[128,2048]{1,0:T(8,128)S(1)}, f32[128,2048]{1,0:T(8,128)}, u32[]{:S(2)}) copy-start(f32[128,2048]{1,0:T(8,128)} %copy-done.3) | copy-start | bytes 3145732
  621.9 74.1 %copy-start.9 = (f32[128,2048]{1,0:T(8,128)S(1)}, f32[128,2048]{1,0:T(8,128)}, u32[]{:S(2)}) copy-start(f32[128,2048]{1,0:T(8,128)} %reduce-scatter.9.cloned.1.call-done) | copy-start | bytes 3145732
  621.9 74.1 %copy-start.13 = (bf16[128,2048]{1,0:T(8,128)(2,1)S(1)}, bf16[128,2048]{1,0:T(8,128)(2,1)}, u32[]{:S(2)}) copy-start(bf16[128,2048]{1,0:T(8,128)(2,1)} %param.33) | copy-start | bytes 1572868
  621.9 74.1 %copy-start.37 = (f32[2048]{0:T(1024)S(1)}, f32[2048]{0:T(1024)}, u32[]{:S(2)}) copy-start(f32[2048]{0:T(1024)} %param.30) | copy-start | bytes 24580
  621.9 74.1 %copy-start.46 = (f32[128]{0:T(128)S(1)}, f32[128]{0:T(128)}, u32[]{:S(2)}) copy-start(f32[128]{0:T(128)} %copy-done.45) | copy-start | bytes 1540
  622.0 74.1 %copy-start.54 = (f32[128]{0:T(128)S(1)}, f32[128]{0:T(128)}, u32[]{:S(2)}) copy-start(f32[128]{0:T(128)} %copy-done.53) | copy-start | bytes 1540
  (65 other events, 668.7 us)
Sparse Core Ops, SparseCore 0:
  11.3 49.8 all-gather.4
  102.5 88.3 reduce-scatter.4
  194.2 45.4 all-gather.6
  241.2 46.0 all-gather.8
  315.8 88.1 reduce-scatter.8
  408.7 45.4 all-gather.10
  555.4 88.3 reduce-scatter.10
  646.6 49.3 reduce-scatter.6
  700.9 513.4 all-reduce.7
  1221.7 178.9 all-reduce.5
where the time goes:
time: 1450 us; the launch traced here: 1440 us
  waiting for transfers between devices  1070 us (74%)
  matrix products  149 us (10%)
  local copies, waits for them, and re-layouts  107 us (7%)
  other arithmetic  46.2 us (3%)
  blocking collectives  40 us (3%)
  between operations  17 us (1%)
    psum x1, waiting for transfers between devices, per_device(): lax.psum((grad_w_query, grad_w_output, grad_w_gate, grad_w_up, grad_w_dow...  515 us
    psum x1, waiting for transfers between devices, per_device(): lax.psum((grad_w_key, grad_w_value, grad_attn_gain, grad_ffn_gain, grad_q...  183 us
    reduce_scatter x1, waiting for transfers between devices, per_device(): lax.psum_scatter(matmul_right_t(grad_gate_up, w_ffn), 'mp', scatter_dimen...  88.1 us
    reduce_scatter x1, waiting for transfers between devices, per_device(): lax.psum_scatter(matmul(context, w_output), 'mp', scatter_dimension=0, ti...  88 us
    all_gather x1, waiting for transfers between devices, per_device(): gathered_one = lax.all_gather(h_one, 'mp', axis=0, tiled=True)  45.7 us
    all_gather x1, waiting for transfers between devices, per_device(): lax.all_gather(grad_mid.astype(jnp.bfloat16), 'mp', axis=0, tiled=True)  44.9 us
    psum x1, blocking collectives, per_device(): lax.psum((grad_w_key, grad_w_value, grad_attn_gain, grad_ffn_gain, grad_q...  40 us
    unnamed x125, local copies, waits for them, and re-layouts  39.9 us
  transfers between devices with their start and end apart: 10, of which 10 were waited for; matrix products, arithmetic and copies ran while one was open for 7% of the time, Pallas kernels for 0%

commit v1 on v0

--- a/solution.py
+++ b/solution.py
@@ -240,10 +240,16 @@
     grad_w_gate = grad_w_ffn[:, :ffn_width]
     grad_w_up = grad_w_ffn[:, ffn_width:]
     summed = lax.psum((grad_w_query, grad_w_output, grad_w_gate, grad_w_up, grad_w_down), "dp")
-    shared = lax.psum(
-        (grad_w_key, grad_w_value, grad_attn_gain, grad_ffn_gain, grad_query_gain, grad_key_gain),
-        ("dp", "mp"),
-    )
+    shared = (
+        grad_w_key,
+        grad_w_value,
+        grad_attn_gain,
+        grad_ffn_gain,
+        grad_query_gain,
+        grad_key_gain,
+    )
+    for over in ("mp", "dp"):
+        shared = lax.psum(shared, over)
     entry_count = tok_count * model_width * lax.axis_size("dp") * lax.axis_size("mp")
     residual_rms = jnp.sqrt(squares_total / entry_count).reshape(1)
     return (

time: 1450 us -> 1570 us (1.083)
  waiting for transfers between devices: 1070 us -> 1180 us
  blocking collectives: 40 us -> 84.6 us
  matrix products: 149 us -> 126 us
    psum x1, waiting for transfers between devices: 515 us -> 623 us  [per_device(): lax.psum((grad_w_query, grad_w_output, grad_w_gate, grad_w_up, grad_w_dow...]
    reduce_scatter x1, waiting for transfers between devices: 21.1 us -> 91.9 us  [per_device(): lax.psum_scatter(matmul_right_t(grad_proj, w_attn), 'mp', scatter_dimensi...]
    psum x1, waiting for transfers between devices: 183 us -> 123 us  [per_device(): shared = lax.psum(shared, over)]
    psum x1 -> x3, blocking collectives: 40 us -> 84.6 us  [the longest x2 44.7 us: per_device(): shared = lax.psum(shared, over)]
    unnamed x125 -> x141, local copies, waits for them, and re-layouts: 39.9 us -> 43.7 us
  transfers between devices with their start and end apart: 10 -> 10, of which waited for: 10 -> 9; matrix products, arithmetic and copies ran while one was open for 7% -> 5% of each run, Pallas kernels for 0% -> 0%
where the time goes in v1:
time: 1570 us; the launch traced here: 1560 us
  waiting for transfers between devices  1180 us (75%)
  matrix products  126 us (8%)
  local copies, waits for them, and re-layouts  104 us (7%)
  blocking collectives  84.6 us (5%)
  other arithmetic  38.4 us (2%)
  between operations  17.1 us (1%)
    psum x1, waiting for transfers between devices, per_device(): lax.psum((grad_w_query, grad_w_output, grad_w_gate, grad_w_up, grad_w_dow...  623 us
    psum x1, waiting for transfers between devices, per_device(): shared = lax.psum(shared, over)  123 us
    reduce_scatter x1, waiting for transfers between devices, per_device(): lax.psum_scatter(matmul_right_t(grad_proj, w_attn), 'mp', scatter_dimensi...  91.9 us
    reduce_scatter x1, waiting for transfers between devices, per_device(): lax.psum_scatter(matmul(context, w_output), 'mp', scatter_dimension=0, ti...  88.4 us
    reduce_scatter x1, waiting for transfers between devices, per_device(): lax.psum_scatter(matmul_right_t(grad_gate_up, w_ffn), 'mp', scatter_dimen...  88.4 us
    all_gather x1, waiting for transfers between devices, per_device(): gathered_one = lax.all_gather(h_one, 'mp', axis=0, tiled=True)  46.9 us
    all_gather x1, waiting for transfers between devices, per_device(): lax.all_gather(grad_mid.astype(jnp.bfloat16), 'mp', axis=0, tiled=True)  45.3 us
    psum x2, blocking collectives, per_device(): shared = lax.psum(shared, over)  44.7 us
  transfers between devices with their start and end apart: 10, of which 9 were waited for; matrix products, arithmetic and copies ran while one was open for 5% of the time, Pallas kernels for 0%

profile of v1, /device:TPU:0, one launch (start us, length us, event | category | flops | bytes accessed | tf_op | source)
XLA Modules:
  0.0 1557.0 jit_solution(9329483233171797584)
XLA Ops:
  14.3 46.9 %all-gather.5.cloned.1.call-done = bf16[1024,2048]{1,0:T(8,128)(2,1)} async-done(((bf16[128,2048]{1,0:T(8,128)(2,1)}), bf16[1024,2048]{1,0:T(8,128)(2,1)}) %all-gather.5.cloned.1.call-update) | async-done | bytes 4194320 | tf_op jit(solution)/shard_map/all_gather | solution.py:92
  68.0 23.7 %while.28 = (s32[]{:T(128)}, bf16[2,512,4,64]{1,3,2,0:T(8,128)(2,1)}, f32[2,4,512]{2,1,0:T(4,128)S(1)}, s32[2]{0:T(128)S(1)}, s32[1024]{0:T(1024)S(1)}, /*index=...) while((s32[]{:T(128)}, ...), condition=%wide.region_6.7_spmd.clone, body=%wide.region_3.6_spmd.clone.sunk | while | flops 563739136 | bytes 32323824 | solution.py:134
  98.2 88.4 %reduce-scatter.5.cloned.1.call-done = f32[128,2048]{1,0:T(8,128)} async-done(((f32[1024,2048]{1,0:T(8,128)}), f32[128,2048]{1,0:T(8,128)}) %reduce-scatter.5.cloned.1.call-update) | async-done | bytes 1048592 | tf_op jit(solution)/shard_map/reduce_scatter | solution.py:136
  197.7 37.7 %all-gather.7.cloned.1.call-done = bf16[1024,2048]{1,0:T(8,128)(2,1)} async-done(((bf16[128,2048]{1,0:T(8,128)(2,1)}), bf16[1024,2048]{1,0:T(8,128)(2,1)}) %all-gather.7.cloned.1.call-update) | async-done | bytes 4194320 | tf_op jit(solution)/shard_map/all_gather | solution.py:142
  235.4 14.9 fusion.103
  250.4 32.4 %all-gather.9.cloned.1.call-done = bf16[1024,2048]{1,0:T(8,128)(2,1)} async-done(((bf16[128,2048]{1,0:T(8,128)(2,1)}), bf16[1024,2048]{1,0:T(8,128)(2,1)}) %all-gather.9.cloned.1.call-update) | async-done | bytes 4194320 | tf_op jit(solution)/shard_map/all_gather | solution.py:162
  282.8 13.1 multiply_convert_fusion.1
  297.9 13.3 fusion.58
  311.3 88.4 %reduce-scatter.9.cloned.1.call-done = f32[128,2048]{1,0:T(8,128)} async-done(((f32[1024,2048]{1,0:T(8,128)}), f32[128,2048]{1,0:T(8,128)}) %reduce-scatter.9.cloned.1.call-update) | async-done | bytes 1048592 | tf_op jit(solution)/shard_map/reduce_scatter | solution.py:169
  404.6 45.3 %all-gather.11.cloned.1.call-done = bf16[1024,2048]{1,0:T(8,128)(2,1)} async-done(((bf16[128,2048]{1,0:T(8,128)(2,1)}), bf16[1024,2048]{1,0:T(8,128)(2,1)}) %all-gather.11.cloned.1.call-update) | async-done | bytes 4194320 | tf_op jit(solution)/shard_map/all_gather | solution.py:174
  454.4 54.9 %while.29 = (s32[]{:T(128)}, f32[1024,64]{0,1:T(8,128)S(1)}, f32[1024,64]{0,1:T(8,128)}, f32[2,512,4,64]{1,0,3,2:T(2,128)}, s32[2]{0:T(128)S(1)}, /*index=5*/s32...) while((s32[]{:T(128)}, f32[1024,64]{0,1:T(8,128)S(1)}, ...), condition=%wide.region_14.15_spmd.clone, body=%wide.region_12.14_spmd.clone.sunk | while | flops 1375664640 | bytes 70195432 | solution.py:209
  470.9 10.4 dynamic_update_slice.30
  498.8 10.4 dynamic_update_slice.30
  545.8 8.2 convolution_convert_fusion
  554.4 10.9 fusion.105
  565.3 11.1 fusion.57
  576.4 6.8 fusion.100
  589.5 123.0 %all-reduce.7.cloned.1.call-done = (f32[2048,512]{1,0:T(8,128)}, f32[2048,512]{1,0:T(8,128)}) async-done(((f32[2048,512]{1,0:T(8,128)}, f32[2048,512]{1,0:T(8,128)}), (f32[2048,512]{1,0:T(8,128)}, f32[2048,512]{1,0:T(8,128)})) %all-reduce.7.cloned.1.call-update) | async-done | bytes 8388624 | tf_op jit(solution)/shard_map/psum | solution.py:252
  713.3 91.9 %reduce-scatter.11.cloned.1.call-done = f32[128,2048]{1,0:T(8,128)} async-done(((f32[1024,2048]{1,0:T(8,128)}), f32[128,2048]{1,0:T(8,128)}) %reduce-scatter.11.cloned.1.call-update) | async-done | bytes 1048592 | tf_op jit(solution)/shard_map/reduce_scatter | solution.py:225
  807.4 39.9 %psum.143 = f32[]{:T(128)} all-reduce(f32[]{:T(128)} %get-tuple-element.288), channel_id=1, replica_groups=mesh['dp'=4,'mp'=8] {'dp','mp'}, use_global_device_ids=true, to_apply=%region_42.43 | all-reduce | flops 1 | bytes 8 | tf_op jit(solution)/shard_map/psum | solution.py:160
  848.0 27.7 %all-reduce = (f32[2048]{0:T(1024)S(1)}, f32[2048]{0:T(1024)S(1)}, f32[64]{0:T(128)S(1)}, f32[64]{0:T(128)S(1)}) all-reduce(f32[2048]{0:T(1024)S(1)} %get-tuple-element.286, f32[2048]{0:T(1024)S(1)} %copy-done.44, f32[64]{0:T(128)S(1)} %reduce_sum.172, f32[64]{0:T(128)S(1)} %get-tuple-element.284), channel_id=1, replica_groups=mesh['dp'=4,'mp'=8] {'mp'}, use_global_device_ids=true, to_apply=%region_29.30 | all-reduce | flops 4224 | bytes 33792 | tf_op jit(solution)/shard_map/psum | solution.py:252
  875.7 17.0 %all-reduce.2 = (f32[2048]{0:T(1024)}, f32[2048]{0:T(1024)}, f32[64]{0:T(128)}, f32[64]{0:T(128)}) all-reduce(f32[2048]{0:T(1024)S(1)} %get-tuple-element.327, f32[2048]{0:T(1024)S(1)} %get-tuple-element.328, f32[64]{0:T(128)S(1)} %get-tuple-element.329, f32[64]{0:T(128)S(1)} %get-tuple-element.330), channel_id=1, replica_groups=mesh['dp'=4,'mp'=8] {'dp'}, use_global_device_ids=true, to_apply=%region_30.31 | all-reduce | flops 4224 | bytes 33792 | tf_op jit(solution)/shard_map/psum | solution.py:252
  896.4 622.6 %all-reduce.9.cloned.1.call-done = (f32[2048,256]{0,1:T(8,128)}, f32[2048,512]{1,0:T(8,128)}, f32[2048,512]{1,0:T(8,128)}, f32[256,2048]{1,0:T(8,128)}, f32[2048...) async-done(((f32[2048,256]{0,1:T(8,128)}, f32[2048,512]{1,0:T(8,128)}, f32[2048,512]{1,0:T(8,128)}, f32[256,2048]{1,0:T(8,128)}, f32[2048,1024]{1,0:T(8,128)}, ...) | async-done | bytes 37748752 | tf_op jit(solution)/shard_map/psum | solution.py:242
  1531.1 9.1 copy.122
  (280 shorter events, 162.3 us)
Async XLA Ops:
  7.2 54.0 %all-gather.5.cloned.1.call-start = ((), (), s32[]{:S(2)}) async-start(), calls=%async_computation.4 | async-start | bytes 4718592 | tf_op jit(solution)/shard_map/all_gather | solution.py:92
  11.2 175.4 %reduce-scatter.5.cloned.1.call-start = ((), (), s32[]{:S(2)}) async-start(), calls=%async_computation.5 | async-start | bytes 9437184 | tf_op jit(solution)/shard_map/reduce_scatter | solution.py:136
  98.1 137.3 %all-gather.7.cloned.1.call-start = ((), (), s32[]{:S(2)}) async-start(), calls=%async_computation.6 | async-start | bytes 4718592 | tf_op jit(solution)/shard_map/all_gather | solution.py:142
  188.6 213.2 %copy-start.2 = (f32[128,2048]{1,0:T(8,128)}, f32[128,2048]{1,0:T(8,128)S(1)}, u32[]{:S(2)}) copy-start(f32[128,2048]{1,0:T(8,128)S(1)} %get-tuple-element.345) | copy-start | bytes 3145732
  188.6 213.2 %copy-start.45 = (f32[128]{0:T(128)}, f32[128]{0:T(128)S(1)}, u32[]{:S(2)}) copy-start(f32[128]{0:T(128)S(1)} %add_rsqrt_fusion.2) | copy-start | bytes 1540
  189.8 93.0 %all-gather.9.cloned.1.call-start = ((), (), s32[]{:S(2)}) async-start(), calls=%async_computation.8 | async-start | bytes 4718592 | tf_op jit(solution)/shard_map/all_gather | solution.py:162
  190.4 209.3 %reduce-scatter.9.cloned.1.call-start = ((), (), s32[]{:S(2)}) async-start(), calls=%async_computation.9 | async-start | bytes 9437184 | tf_op jit(solution)/shard_map/reduce_scatter | solution.py:169
  311.2 90.6 %copy-start.9 = (bf16[128,2048]{1,0:T(8,128)(2,1)S(1)}, bf16[128,2048]{1,0:T(8,128)(2,1)}, u32[]{:S(2)}) copy-start(bf16[128,2048]{1,0:T(8,128)(2,1)} %param.33) | copy-start | bytes 1572868
  311.2 93.2 %copy-start.54 = (f32[64]{0:T(128)S(1)}, f32[64]{0:T(128)}, u32[]{:S(2)}) copy-start(f32[64]{0:T(128)} %param.31) | copy-start | bytes 772
  311.3 138.6 %all-gather.11.cloned.1.call-start = ((), (), s32[]{:S(2)}) async-start(), calls=%async_computation.10 | async-start | bytes 4718592 | tf_op jit(solution)/shard_map/all_gather | solution.py:174
  404.2 308.3 %all-reduce.7.cloned.1.call-start = ((), (), s32[]{:S(2)}) async-start(), calls=%async_computation.12 | async-start | bytes 16777216 | tf_op jit(solution)/shard_map/psum | solution.py:252
  536.5 268.6 %reduce-scatter.11.cloned.1.call-start = ((), (), s32[]{:S(2)}) async-start(), calls=%async_computation.11 | async-start | bytes 9437184 | tf_op jit(solution)/shard_map/reduce_scatter | solution.py:225
  544.2 348.5 %reduce-scatter.7.cloned.1.call-start = ((), (), s32[]{:S(2)}) async-start(), calls=%async_computation.7 | async-start | bytes 4718592 | tf_op jit(solution)/shard_map/reduce_scatter | solution.py:149
  554.0 965.0 %all-reduce.9.cloned.1.call-start = ((), (), s32[]{:S(2)}) async-start(), calls=%async_computation.13 | async-start | bytes 75497472 | tf_op jit(solution)/shard_map/psum | solution.py:242
  712.5 92.6 %copy-start.7 = (bf16[128,2048]{1,0:T(8,128)(2,1)S(1)}, bf16[128,2048]{1,0:T(8,128)(2,1)}, u32[]{:S(2)}) copy-start(bf16[128,2048]{1,0:T(8,128)(2,1)} %param.19) | copy-start | bytes 1572868
  712.5 92.6 %copy-start.39 = (f32[2048]{0:T(1024)S(1)}, f32[2048]{0:T(1024)}, u32[]{:S(2)}) copy-start(f32[2048]{0:T(1024)} %param.29) | copy-start | bytes 24580
  712.5 92.6 %copy-start.48 = (f32[128]{0:T(128)S(1)}, f32[128]{0:T(128)}, u32[]{:S(2)}) copy-start(f32[128]{0:T(128)} %copy-done.47) | copy-start | bytes 1540
  712.5 135.5 %copy-start.44 = (f32[2048]{0:T(1024)S(1)}, f32[2048]{0:T(1024)}, u32[]{:S(2)}) copy-start(f32[2048]{0:T(1024)} %get-tuple-element.282) | copy-start | bytes 24580
  712.5 180.2 %copy-start.3 = (f32[128,2048]{1,0:T(8,128)S(1)}, f32[128,2048]{1,0:T(8,128)}, u32[]{:S(2)}) copy-start(f32[128,2048]{1,0:T(8,128)} %copy-done.2) | copy-start | bytes 3145732
  712.5 180.2 %copy-start.8 = (f32[128,2048]{1,0:T(8,128)S(1)}, f32[128,2048]{1,0:T(8,128)}, u32[]{:S(2)}) copy-start(f32[128,2048]{1,0:T(8,128)} %reduce-scatter.9.cloned.1.call-done) | copy-start | bytes 3145732
  712.5 180.2 %copy-start.10 = (bf16[128,2048]{1,0:T(8,128)(2,1)S(1)}, bf16[128,2048]{1,0:T(8,128)(2,1)}, u32[]{:S(2)}) copy-start(bf16[128,2048]{1,0:T(8,128)(2,1)} %param.33) | copy-start | bytes 1572868
  712.5 180.2 %copy-start.38 = (f32[2048]{0:T(1024)S(1)}, f32[2048]{0:T(1024)}, u32[]{:S(2)}) copy-start(f32[2048]{0:T(1024)} %param.30) | copy-start | bytes 24580
  712.6 180.2 %copy-start.46 = (f32[128]{0:T(128)S(1)}, f32[128]{0:T(128)}, u32[]{:S(2)}) copy-start(f32[128]{0:T(128)} %copy-done.45) | copy-start | bytes 1540
  712.6 180.2 %copy-start.56 = (f32[128]{0:T(128)S(1)}, f32[128]{0:T(128)}, u32[]{:S(2)}) copy-start(f32[128]{0:T(128)} %copy-done.55) | copy-start | bytes 1540
  (55 other events, 839.9 us)
Sparse Core Ops, SparseCore 0:
  11.3 49.8 all-gather.4
  98.2 88.3 reduce-scatter.4
  189.9 45.4 all-gather.6
  236.9 45.8 all-gather.8
  311.4 88.2 reduce-scatter.8
  404.3 45.4 all-gather.10
  536.6 175.8 all-reduce.6
  715.4 89.7 reduce-scatter.10
  808.0 49.4 reduce-scatter.6
  862.7 656.2 all-reduce.8
